TPU v7x, 32 devices: a whole 2x2x4 slice. The times are simulated.
32 devices in a mesh: orb: 16 (over z, x, core), aux: 2 (over y).
Axes of the slice: x: 2, y: 2, z: 4, core: 2. Of those that a mesh axis runs over, the one named last changes fastest.
Arguments:
- three_index: float32 [56, 1024, 2048], P(None, 'aux', 'orb'), may hold values from -0.5 to 0.5
- pair_density: float32 [3136, 3136], P('orb'), as said below
- active_orbitals: int32 [56], replicated, may hold values from 200 to 2047, as said below
- screen_mask: int32 [64, 128], P('aux', 'orb'), may hold values from 0 to 1
- one_density: float32 [56, 56], replicated
- inactive_fock: float32 [2048, 256], P('orb'), may hold values from -6 to 6
- active_fock: float32 [2048, 200], P('orb'), may hold values from -6 to 6
Outputs:
- rotation_gradient: float32 [2048, 256], P(('orb', 'aux'))
Inputs may be any that keep to these rules, and one draw needn't show every extreme that they name: `active_orbitals`: 56 distinct orbital indices. pair_density is symmetric: its entry at (tu, vw) equals that at (vw, tu).
All inputs are finite; a program needn't handle non-finite values.
Results may differ from a plain program's by a relative error of at most 0.0001.
Values sent between devices are 32-bit elements; how exact they have to be, the bound alone decides.
No kernel may reach another device: no remote copies, remote signals or barrier semaphores. Data moves between devices by JAX's collectives and lax.ppermute only.
A program may use at most 128 MiB of HBM per device.

v0:
```python
import jax
import jax.numpy as jnp
from jax import lax
from jax.sharding import PartitionSpec as P


def shards(
    three_index, pair_density, active_orbitals, screen_mask, one_density, inactive_fock, active_fock
):
    highest = lax.Precision.HIGHEST
    act_count = three_index.shape[0]
    slab_count = three_index.shape[1]
    row_count = three_index.shape[2]
    inactive_count = active_fock.shape[1]
    orb_position = lax.axis_index("orb")
    kept_mask = jnp.repeat(
        jnp.repeat(screen_mask.astype(jnp.float32), slab_count // screen_mask.shape[0], axis=0),
        row_count // screen_mask.shape[1],
        axis=1,
    )
    screened = three_index * kept_mask[None]
    global_rows = orb_position * row_count + jnp.arange(row_count, dtype=jnp.int32)
    active_pick = (global_rows[:, None] == active_orbitals[None, :]).astype(jnp.float32)
    partial_pairs = jnp.einsum("wPp,pv->Pvw", screened, active_pick, precision=highest).reshape(
        slab_count, act_count * act_count
    )
    pairs = lax.psum(partial_pairs, "orb")
    column_block = jnp.dot(pairs, pair_density.T, precision=highest)
    half = lax.all_gather(column_block, "orb", axis=1, tiled=True)
    q_partial = jnp.einsum(
        "uPp,Ptu->pt", screened, half.reshape(slab_count, act_count, act_count), precision=highest
    )
    occ_index = jnp.concatenate([jnp.arange(inactive_count, dtype=jnp.int32), active_orbitals])
    row_share = row_count // lax.axis_size("aux")
    aux_offset = lax.axis_index("aux") * row_share
    qmatrix = lax.psum(q_partial, "aux")
    inactive_cols = 2.0 * (inactive_fock[:, :inactive_count] + active_fock)
    active_cols = (
        jnp.dot(inactive_fock[:, inactive_count:], one_density, precision=highest) + qmatrix
    )
    fock = jnp.concatenate([inactive_cols, active_cols], axis=1)
    occ_pick = (global_rows[:, None] == occ_index[None, :]).astype(jnp.float32)
    occupied = lax.psum(jnp.dot(occ_pick.T, fock, precision=highest), "orb")
    fock_mine = lax.dynamic_slice_in_dim(fock, aux_offset, row_share, 0)
    pick_mine = lax.dynamic_slice_in_dim(occ_pick, aux_offset, row_share, 0)
    transposed = jnp.dot(pick_mine, occupied.T, precision=highest)
    return 2.0 * (fock_mine - transposed)


def solution(mesh):
    in_specs = (
        P(None, "aux", "orb"),
        P("orb", None),
        P(),
        P("aux", "orb"),
        P(),
        P("orb", None),
        P("orb", None),
    )
    out_specs = P(("orb", "aux"), None)
    return jax.shard_map(shards, mesh=mesh, in_specs=in_specs, out_specs=out_specs, check_vma=False)
```

profile of v0, /device:TPU:1, one launch (start us, length us, event | category | flops | bytes accessed | tf_op | source)
XLA Modules:
  0.0 370.7 jit_solution(4190907556177980599)
XLA Ops:
  6.5 0.0 copy-start
  6.5 0.0 all-reduce.3.cloned.1.call-start
  6.5 0.8 convert_element_type.2
  7.4 0.1 broadcast_in_dim.4
  7.5 0.1 reshape.16
  7.6 0.1 copy.22
  7.8 13.5 %fusion.7 = f32[512,56,56]{0,1,2:T(8,128)S(1)} fusion(f32[56,512,128]{2,1,0:T(8,128)} %param.7, f32[512,128]{1,0:T(8,128)S(1)} %copy.22, s32[128]{0:T(128)S(1)} %iota_add_fusion, s32[56]{0:T(128)} %param.9), kind=kOutput, calls=%fused_computation.7 | convolution fusion | flops 2469927936 | bytes 21365472 | tf_op jit(solution)/shard_map/wPp,pv->Pvw/dot_general | solution.py:24
  21.2 6.4 %copy.23 = f32[512,56,56]{0,2,1:T(8,128)} copy(f32[512,56,56]{0,1,2:T(8,128)S(1)} %fusion.7) | data formatting | bytes 12845056 | tf_op jit(solution)/shard_map/wPp,pv->Pvw/transpose | solution.py:24
  27.6 0.0 all-reduce.3.cloned.1.call-update
  27.6 0.0 copy-start.2
  27.6 0.0 copy-start.4
  27.6 0.0 copy-start.1
  27.7 0.2 all-gather.3.cloned.1.call-start
  27.9 143.9 %all-reduce.3.cloned.1.call-done = f32[512,3136]{0,1:T(8,128)} async-done(((f32[512,3136]{0,1:T(8,128)}), f32[512,3136]{0,1:T(8,128)}) %all-reduce.3.cloned.1.call-update) | async-done | bytes 6422544 | tf_op jit(solution)/shard_map/psum | solution.py:27
  171.8 0.0 copy-done
  171.8 8.6 %convolution_bitcast_fusion = f32[1,196,512]{2,1,0:T(8,128)} fusion(f32[512,3136]{0,1:T(8,128)} %all-reduce.3.cloned.1.call-done, f32[196,3136]{1,0:T(8,128)S(1)} %copy-done), kind=kOutput, calls=%fused_computation.8 | convolution fusion | flops 3776446464 | bytes 9282560 | tf_op jit(solution)/shard_map/dot_general | solution.py:28
  180.4 0.0 all-gather.3.cloned.1.call-update
  180.4 0.0 all-reduce.5.cloned.1.call-start
  180.5 0.0 copy-done.2
  180.5 0.1 copy.21
  180.6 0.0 copy-done.4
  180.6 0.1 pad_add_fusion
  180.7 0.0 copy-done.1
  180.7 63.3 %all-gather.3.cloned.1.call-done = f32[16,196,512]{2,1,0:T(8,128)} async-done(((f32[1,196,512]{2,1,0:T(8,128)}), f32[16,196,512]{2,1,0:T(8,128)}) %all-gather.3.cloned.1.call-update) | async-done | bytes 6422544 | tf_op jit(solution)/shard_map/all_gather | solution.py:29
  244.0 6.1 %reshape.20 = f32[3136,512]{1,0:T(8,128)} reshape(f32[16,196,512]{2,1,0:T(8,128)} %all-gather.3.cloned.1.call-done) | data formatting | bytes 12845056
  250.2 0.0 copy-start.3
  250.2 15.4 %fusion.11 = f32[128,56]{0,1:T(8,128)S(1)} fusion(f32[512,56,56]{0,2,1:T(8,128)} %bitcast.23, f32[56,512,128]{2,1,0:T(8,128)} %param.7, f32[512,128]{1,0:T(8,128)S(1)} %copy.22), kind=kOutput, calls=%fused_computation.11 | convolution fusion | flops 2469920768 | bytes 21393408 | tf_op jit(solution)/shard_map/uPp,Ptu->pt/dot_general | solution.py:30
  265.5 6.3 %psum.22 = f32[128,56]{0,1:T(8,128)S(1)} all-reduce(f32[128,56]{0,1:T(8,128)S(1)} %fusion.11), channel_id=1, replica_groups=mesh['orb'=16,'aux'=2] {'aux'}, use_global_device_ids=true, to_apply=%region_1.0 | all-reduce | flops 7168 | bytes 57344 | tf_op jit(solution)/shard_map/psum | solution.py:36
  271.8 0.0 copy-done.3
  271.8 0.3 convolution_add_fusion
  272.2 0.1 copy.25
  272.3 1.1 fusion.16
  273.4 0.0 all-reduce.5.cloned.1.call-update
  273.4 0.1 broadcast_compare_fusion
  273.5 88.9 %all-reduce.5.cloned.1.call-done = f32[256,256]{1,0:T(8,128)} async-done(((f32[256,256]{1,0:T(8,128)}), f32[256,256]{1,0:T(8,128)}) %all-reduce.5.cloned.1.call-update) | async-done | bytes 262160 | tf_op jit(solution)/shard_map/psum | solution.py:43
  362.3 1.9 fusion.10
  (4 shorter events, 0.0 us)
Async XLA Ops:
  6.5 165.2 %copy-start = (f32[196,3136]{1,0:T(8,128)S(1)}, f32[196,3136]{1,0:T(8,128)}, u32[]{:S(2)}) copy-start(f32[196,3136]{1,0:T(8,128)} %param.8) | copy-start | bytes 7375876
  6.5 165.2 %all-reduce.3.cloned.1.call-start = ((), (), s32[]{:S(2)}) async-start(), calls=%async_computation | async-start | bytes 12845056 | tf_op jit(solution)/shard_map/psum | solution.py:27
  27.6 152.8 %copy-start.2 = (f32[128,200]{0,1:T(8,128)S(1)}, f32[128,200]{0,1:T(8,128)}, u32[]{:S(2)}) copy-start(f32[128,200]{0,1:T(8,128)} %param.13) | copy-start | bytes 307204
  27.6 153.0 %copy-start.4 = (s32[56]{0:T(128)S(1)}, s32[56]{0:T(128)}, u32[]{:S(2)}) copy-start(s32[56]{0:T(128)} %param.9) | copy-start | bytes 676
  27.6 153.0 %copy-start.1 = (f32[128,256]{1,0:T(8,128)S(1)}, f32[128,256]{1,0:T(8,128)}, u32[]{:S(2)}) copy-start(f32[128,256]{1,0:T(8,128)} %param.12) | copy-start | bytes 393220
  27.7 216.4 %all-gather.3.cloned.1.call-start = ((), (), s32[]{:S(2)}) async-start(), calls=%async_computation.2 | async-start | bytes 6963200 | tf_op jit(solution)/shard_map/all_gather | solution.py:29
  180.4 181.9 %all-reduce.5.cloned.1.call-start = ((), (), s32[]{:S(2)}) async-start(), calls=%async_computation.1 | async-start | bytes 524288 | tf_op jit(solution)/shard_map/psum | solution.py:43
  250.2 21.7 %copy-start.3 = (f32[56,56]{1,0:T(8,128)S(1)}, f32[56,56]{1,0:T(8,128)}, u32[]{:S(2)}) copy-start(f32[56,56]{1,0:T(8,128)} %param.11) | copy-start | bytes 37636
Sparse Core Ops, SparseCore 0:
  27.7 143.9 all-reduce.2
  180.5 63.4 all-gather.2
  273.5 88.8 all-reduce.4
where the time goes:
time: 371 us
  waiting for transfers between devices  296 us (80%)
  matrix products  40.7 us (11%)
  between operations  13.2 us (4%)
  local copies, waits for them, and re-layouts  13 us (4%)
  blocking collectives  6.31 us (2%)
    psum x1, waiting for transfers between devices, shards(): pairs = lax.psum(partial_pairs, 'orb')  144 us
    psum x1, waiting for transfers between devices, shards(): occupied = lax.psum(jnp.dot(occ_pick.T, fock, precision=highest), 'orb')  88.9 us
    all_gather x1, waiting for transfers between devices, shards(): half = lax.all_gather(column_block, 'orb', axis=1, tiled=True)  63.3 us
    dot_general x1, matrix products, shards(): jnp.einsum('uPp,Ptu->pt', screened, half.reshape(slab_count, act_count, a...  15.4 us
    dot_general x1, matrix products, shards(): jnp.einsum('wPp,pv->Pvw', screened, active_pick, precision=highest)  13.5 us
    dot_general x1, matrix products, shards(): column_block = jnp.dot(pairs, pair_density.T, precision=highest)  8.61 us
  transfers between devices with their start and end apart: 3, of which 3 were waited for; matrix products, arithmetic and copies ran while one was open for 0% of the time, Pallas kernels for 0%

commit v1 on v0

--- a/solution.py
+++ b/solution.py
@@ -2,6 +2,12 @@
 import jax.numpy as jnp
 from jax import lax
 from jax.sharding import PartitionSpec as P
+
+
+def gather_and_add(x, axis):
+    pieces = lax.all_gather(x, axis, axis=0, tiled=False)
+    summed = pieces.sum(axis=0)
+    return summed
 
 
 def shards(
@@ -40,7 +46,7 @@
     )
     fock = jnp.concatenate([inactive_cols, active_cols], axis=1)
     occ_pick = (global_rows[:, None] == occ_index[None, :]).astype(jnp.float32)
-    occupied = lax.psum(jnp.dot(occ_pick.T, fock, precision=highest), "orb")
+    occupied = gather_and_add(jnp.dot(occ_pick.T, fock, precision=highest), "orb")
     fock_mine = lax.dynamic_slice_in_dim(fock, aux_offset, row_share, 0)
     pick_mine = lax.dynamic_slice_in_dim(occ_pick, aux_offset, row_share, 0)
     transposed = jnp.dot(pick_mine, occupied.T, precision=highest)

time: 371 us -> 334 us (0.900)
  waiting for transfers between devices: 296 us -> 258 us
    psum x1 -> x0, waiting for transfers between devices: 88.9 us -> none  [shards(): occupied = lax.psum(jnp.dot(occ_pick.T, fock, precision=highest), 'orb')]
    all_gather x0 -> x1, waiting for transfers between devices: none -> 50.3 us  [gather_and_add(): pieces = lax.all_gather(x, axis, axis=0, tiled=False)]
where the time goes in v1:
time: 334 us
  waiting for transfers between devices  258 us (77%)
  matrix products  39.8 us (12%)
  between operations  13.2 us (4%)
  local copies, waits for them, and re-layouts  13 us (4%)
  blocking collectives  6.31 us (2%)
  other arithmetic  3.51 us (1%)
    psum x1, waiting for transfers between devices, shards(): pairs = lax.psum(partial_pairs, 'orb')  144 us
    all_gather x1, waiting for transfers between devices, shards(): half = lax.all_gather(column_block, 'orb', axis=1, tiled=True)  63.4 us
    all_gather x1, waiting for transfers between devices, gather_and_add(): pieces = lax.all_gather(x, axis, axis=0, tiled=False)  50.3 us
    dot_general x1, matrix products, shards(): jnp.einsum('uPp,Ptu->pt', screened, half.reshape(slab_count, act_count, a...  15.4 us
    dot_general x1, matrix products, shards(): jnp.einsum('wPp,pv->Pvw', screened, active_pick, precision=highest)  13.5 us
    dot_general x1, matrix products, shards(): column_block = jnp.dot(pairs, pair_density.T, precision=highest)  8.61 us
  transfers between devices with their start and end apart: 3, of which 3 were waited for; matrix products, arithmetic and copies ran while one was open for 0% of the time, Pallas kernels for 0%

profile of v1, /device:TPU:1, one launch (start us, length us, event | category | flops | bytes accessed | tf_op | source)
XLA Modules:
  0.0 333.7 jit_solution(12978675800703933862)
XLA Ops:
  6.5 0.0 copy-start
  6.5 0.0 all-reduce.2.cloned.1.call-start
  6.5 0.8 convert_element_type.2
  7.4 0.1 broadcast_in_dim.4
  7.5 0.1 reshape.16
  7.6 0.1 copy.22
  7.8 13.5 %fusion.7 = f32[512,56,56]{0,1,2:T(8,128)S(1)} fusion(f32[56,512,128]{2,1,0:T(8,128)} %param.7, f32[512,128]{1,0:T(8,128)S(1)} %copy.22, s32[128]{0:T(128)S(1)} %iota_add_fusion, s32[56]{0:T(128)} %param.9), kind=kOutput, calls=%fused_computation.7 | convolution fusion | flops 2469927936 | bytes 21365472 | tf_op jit(solution)/shard_map/wPp,pv->Pvw/dot_general | solution.py:30
  21.2 6.4 %copy.23 = f32[512,56,56]{0,2,1:T(8,128)} copy(f32[512,56,56]{0,1,2:T(8,128)S(1)} %fusion.7) | data formatting | bytes 12845056 | tf_op jit(solution)/shard_map/wPp,pv->Pvw/transpose | solution.py:30
  27.6 0.0 all-reduce.2.cloned.1.call-update
  27.6 0.0 copy-start.2
  27.6 0.0 copy-start.4
  27.6 0.0 copy-start.1
  27.7 0.2 all-gather.7.cloned.1.call-start
  27.9 143.9 %all-reduce.2.cloned.1.call-done = f32[512,3136]{0,1:T(8,128)} async-done(((f32[512,3136]{0,1:T(8,128)}), f32[512,3136]{0,1:T(8,128)}) %all-reduce.2.cloned.1.call-update) | async-done | bytes 6422544 | tf_op jit(solution)/shard_map/psum | solution.py:33
  171.8 0.0 copy-done
  171.8 8.6 %convolution_bitcast_fusion = f32[1,196,512]{2,1,0:T(8,128)} fusion(f32[512,3136]{0,1:T(8,128)} %all-reduce.2.cloned.1.call-done, f32[196,3136]{1,0:T(8,128)S(1)} %copy-done), kind=kOutput, calls=%fused_computation.8 | convolution fusion | flops 3776446464 | bytes 9282560 | tf_op jit(solution)/shard_map/dot_general | solution.py:34
  180.4 0.0 all-gather.7.cloned.1.call-update
  180.4 0.0 all-gather.5.cloned.1.call-start
  180.5 0.0 copy-done.2
  180.5 0.1 copy.21
  180.6 0.0 copy-done.4
  180.6 0.1 pad_add_fusion
  180.7 0.0 copy-done.1
  180.7 63.4 %all-gather.7.cloned.1.call-done = f32[16,196,512]{2,1,0:T(8,128)} async-done(((f32[1,196,512]{2,1,0:T(8,128)}), f32[16,196,512]{2,1,0:T(8,128)}) %all-gather.7.cloned.1.call-update) | async-done | bytes 6422544 | tf_op jit(solution)/shard_map/all_gather | solution.py:35
  244.0 6.1 %reshape.21 = f32[3136,512]{1,0:T(8,128)} reshape(f32[16,196,512]{2,1,0:T(8,128)} %all-gather.7.cloned.1.call-done) | data formatting | bytes 12845056
  250.2 0.0 copy-start.3
  250.2 15.4 %fusion.11 = f32[128,56]{0,1:T(8,128)S(1)} fusion(f32[512,56,56]{0,2,1:T(8,128)} %bitcast.24, f32[56,512,128]{2,1,0:T(8,128)} %param.7, f32[512,128]{1,0:T(8,128)S(1)} %copy.22), kind=kOutput, calls=%fused_computation.11 | convolution fusion | flops 2469920768 | bytes 21393408 | tf_op jit(solution)/shard_map/uPp,Ptu->pt/dot_general | solution.py:36
  265.5 6.3 %psum.15 = f32[128,56]{0,1:T(8,128)S(1)} all-reduce(f32[128,56]{0,1:T(8,128)S(1)} %fusion.11), channel_id=1, replica_groups=mesh['orb'=16,'aux'=2] {'aux'}, use_global_device_ids=true, to_apply=%region_1.0 | all-reduce | flops 7168 | bytes 57344 | tf_op jit(solution)/shard_map/psum | solution.py:42
  271.8 0.0 copy-done.3
  271.8 0.3 convolution_add_fusion
  272.2 0.1 copy.25
  272.3 1.1 fusion.16
  273.4 0.0 all-gather.5.cloned.1.call-update
  273.4 0.1 broadcast_compare_fusion
  273.5 50.3 %all-gather.5.cloned.1.call-done = f32[4096,256]{1,0:T(8,128)} async-done(((f32[256,256]{1,0:T(8,128)}), f32[4096,256]{1,0:T(8,128)}) %all-gather.5.cloned.1.call-update) | async-done | bytes 4194320 | tf_op jit(solution)/shard_map/all_gather | solution.py:8
  323.8 2.5 reduce_sum.9
  326.3 0.9 fusion.10
  (4 shorter events, 0.0 us)
Async XLA Ops:
  6.5 165.2 %copy-start = (f32[196,3136]{1,0:T(8,128)S(1)}, f32[196,3136]{1,0:T(8,128)}, u32[]{:S(2)}) copy-start(f32[196,3136]{1,0:T(8,128)} %param.8) | copy-start | bytes 7375876
  6.5 165.2 %all-reduce.2.cloned.1.call-start = ((), (), s32[]{:S(2)}) async-start(), calls=%async_computation | async-start | bytes 12845056 | tf_op jit(solution)/shard_map/psum | solution.py:33
  27.6 152.8 %copy-start.2 = (f32[128,200]{0,1:T(8,128)S(1)}, f32[128,200]{0,1:T(8,128)}, u32[]{:S(2)}) copy-start(f32[128,200]{0,1:T(8,128)} %param.13) | copy-start | bytes 307204
  27.6 153.0 %copy-start.4 = (s32[56]{0:T(128)S(1)}, s32[56]{0:T(128)}, u32[]{:S(2)}) copy-start(s32[56]{0:T(128)} %param.9) | copy-start | bytes 676
  27.6 153.0 %copy-start.1 = (f32[128,256]{1,0:T(8,128)S(1)}, f32[128,256]{1,0:T(8,128)}, u32[]{:S(2)}) copy-start(f32[128,256]{1,0:T(8,128)} %param.12) | copy-start | bytes 393220
  27.7 216.4 %all-gather.7.cloned.1.call-start = ((), (), s32[]{:S(2)}) async-start(), calls=%async_computation.2 | async-start | bytes 6963200 | tf_op jit(solution)/shard_map/all_gather | solution.py:35
  180.4 143.4 %all-gather.5.cloned.1.call-start = ((), (), s32[]{:S(2)}) async-start(), calls=%async_computation.1 | async-start | bytes 4456448 | tf_op jit(solution)/shard_map/all_gather | solution.py:8
  250.2 21.7 %copy-start.3 = (f32[56,56]{1,0:T(8,128)S(1)}, f32[56,56]{1,0:T(8,128)}, u32[]{:S(2)}) copy-start(f32[56,56]{1,0:T(8,128)} %param.11) | copy-start | bytes 37636
Sparse Core Ops, SparseCore 0:
  27.7 143.9 all-reduce.1
  180.5 63.4 all-gather.6
  273.5 50.2 all-gather.4
